TPU v7x, 32 devices: a whole 2x2x4 slice. The times are simulated.
32 devices in a mesh: cols: 4 (over y, x), rows: 8 (over z, core).
Axes of the slice: x: 2, y: 2, z: 4, core: 2. Of those that a mesh axis runs over, the one named last changes fastest.
Arguments:
- gradient: float32 [128, 8192], P('cols', 'rows'), may hold values from -100 to 100
- width_factor: float32 [128, 128], P(None, 'cols'), may hold values from -3 to 4, as said below
- diag_blocks: float32 [64, 128, 128], P('rows'), may hold values from -2 to 24, as said below
- jacobi_inverse: float32 [64, 128, 128], P('rows'), may hold values from -2 to 2, as said below
- coupling_tiles: bfloat16 [32, 128, 128], P('rows'), may hold values from -4 to 4, as said below
- tile_local: int32 [32], P('rows'), may hold values from 0 to 7
- tile_remote: int32 [32], P('rows'), may hold values from 0 to 63, as said below
- tile_count: int32 [8], P('rows'), may hold values from 0 to 3, as said below
Outputs:
- solution: float32 [128, 8192], P('cols', 'rows')
- residual: float32 [128, 8192], P('cols', 'rows')
Inputs may be any that keep to these rules, and one draw needn't show every extreme that they name: `tile_remote`: the live entries are the first tile_count entries of each device's list; they name distinct devices other than the owner, each at most once. For a live entry of device d naming block J of device e, device e has a live entry naming d's block with its tile the transpose. Pad entries hold valid indices. `tile_count`: at most 3 on one device, reached on some device. `coupling_tiles`: with diag_blocks and the live entries, M is symmetric positive definite. `diag_blocks`: symmetric positive definite tiles. `jacobi_inverse`: the inverses of diag_blocks, symmetric. `width_factor`: symmetric positive definite.
All inputs are finite; a program needn't handle non-finite values.
Results may differ from a plain program's by a relative error of at most 0.0085.
Values may be sent and summed in bfloat16 or wider, within the bound.
No kernel may reach another device: no remote copies, remote signals or barrier semaphores. Data moves between devices by JAX's collectives and lax.ppermute only.
A program may use at most 64 MiB of HBM per device.

v0:
```python
import jax
import jax.numpy as jnp
from jax import lax
from jax.sharding import PartitionSpec as P

BLOCK = 128
ITERS = 6
highest = lax.Precision.HIGHEST


def on_device(
    gradient,
    width_factor,
    diag_blocks,
    jacobi_inverse,
    coupling_tiles,
    tile_local,
    tile_remote,
    tile_count,
):
    width_dev, rows_dev = gradient.shape
    blocks_dev = diag_blocks.shape[0]
    slot_count = tile_local.shape[0]
    devices = lax.axis_size("rows")
    active_slot = jnp.arange(slot_count, dtype=jnp.int32) < tile_count[0]
    placing = (
        (tile_local[:, None] == jnp.arange(blocks_dev, dtype=jnp.int32)[None, :])
        & active_slot[:, None]
    ).astype(jnp.float32)
    owner_dev = tile_remote // blocks_dev
    matches = active_slot[:, None] & (
        owner_dev[:, None] == jnp.arange(devices, dtype=jnp.int32)[None, :]
    )
    request = jnp.sum(jnp.where(matches, (tile_remote % blocks_dev)[:, None], 0), axis=0)
    granted = lax.all_to_all(request, "rows", split_axis=0, concat_axis=0, tiled=True)

    def precondition(vector):
        blocks = vector.reshape(width_dev, blocks_dev, BLOCK)
        return jnp.einsum("enj,nji->eni", blocks, jacobi_inverse, precision=highest).reshape(
            width_dev, rows_dev
        )

    solution = jnp.zeros_like(gradient)
    residual = gradient
    precond_res = precondition(residual)
    direction = precond_res
    res_norm = lax.psum(jnp.sum(residual * precond_res), ("cols", "rows"))
    for iteration in range(ITERS):
        apply_blocks = direction.reshape(width_dev, blocks_dev, BLOCK)
        local_part = jnp.einsum("enj,nji->eni", apply_blocks, diag_blocks, precision=highest)
        rounded = direction.astype(jnp.bfloat16).reshape(width_dev, blocks_dev, BLOCK)
        incoming = lax.all_to_all(
            rounded[:, granted, :], "rows", split_axis=1, concat_axis=1, tiled=True
        )
        sources = incoming[:, owner_dev, :]
        products = jnp.einsum(
            "ekj,kji->eki", sources, coupling_tiles, preferred_element_type=jnp.float32
        )
        coupled = jnp.einsum("eki,kb->ebi", products, placing, precision=highest)
        summed = lax.psum(
            jnp.dot(
                width_factor, (local_part + coupled).reshape(width_dev, rows_dev), precision=highest
            ),
            "cols",
        )
        fisher_dir = lax.dynamic_slice_in_dim(
            summed, lax.axis_index("cols") * width_dev, width_dev, 0
        )
        precond_fisher = precondition(fisher_dir)
        curvature, cross_term, second_term = lax.psum(
            (
                jnp.sum(direction * fisher_dir),
                jnp.sum(fisher_dir * precond_res),
                jnp.sum(fisher_dir * precond_fisher),
            ),
            ("cols", "rows"),
        )
        step_size = res_norm / curvature
        solution = solution + step_size * direction
        residual = residual - step_size * fisher_dir
        if iteration + 1 < ITERS:
            precond_res = precond_res - step_size * precond_fisher
            next_norm = (
                res_norm - 2.0 * step_size * cross_term + step_size * step_size * second_term
            )
            direction = precond_res + next_norm / res_norm * direction
            res_norm = next_norm
    return (solution, residual)


def solution(mesh):
    placed = (
        P("cols", "rows"),
        P(None, "cols"),
        P("rows", None, None),
        P("rows", None, None),
        P("rows", None, None),
        P("rows"),
        P("rows"),
        P("rows"),
    )
    return jax.shard_map(
        on_device,
        mesh=mesh,
        in_specs=placed,
        out_specs=(P("cols", "rows"), P("cols", "rows")),
        check_vma=False,
    )
```

profile of v0, /device:TPU:0, one launch (start us, length us, event | category | flops | bytes accessed | tf_op | source)
XLA Modules:
  0.0 644.4 jit_solution(5383939424549361704)
XLA Ops:
  7.9 0.6 copy-done.6
  8.6 0.7 copy.175
  9.3 6.4 all-to-all-start
  15.7 1.5 bitcast_convert_fusion
  17.2 4.0 all-to-all-done
  21.4 1.2 gather_fusion
  22.6 3.4 all-to-all-start.1
  26.1 5.7 all-to-all-done.1
  31.8 0.6 gather_fusion.1
  32.6 0.3 fusion.73
  32.8 0.6 fusion.5
  33.6 1.4 convolution_bitcast_fusion.5
  35.1 44.0 %all-reduce.12.cloned.1.call-done = f32[128,1024]{1,0:T(8,128)} async-done(((f32[128,1024]{1,0:T(8,128)}), f32[128,1024]{1,0:T(8,128)}) %all-reduce.12.cloned.1.call-update) | async-done | bytes 524304 | tf_op jit(solution)/shard_map/psum | solution.py:60
  79.0 1.5 fusion.49
  80.5 1.6 fusion.25
  82.1 39.6 %all-reduce.4 = (f32[]{:T(128)}, f32[]{:T(128)}, f32[]{:T(128)}) all-reduce(f32[]{:T(128)} %get-tuple-element.24, f32[]{:T(128)} %get-tuple-element.23, f32[]{:T(128)} %get-tuple-element.22), channel_id=1, replica_groups=mesh['cols'=4,'rows'=8] {'cols','rows'}, use_global_device_ids=true, to_apply=%region_1.2 | all-reduce | flops 3 | bytes 24 | tf_op jit(solution)/shard_map/psum | solution.py:47
  125.5 0.6 gather_fusion.2
  126.0 9.3 %all_to_all.42 = bf16[32,8,128]{2,0,1:T(8,128)(2,1)S(1)} all-to-all(bf16[32,8,128]{2,0,1:T(8,128)(2,1)S(1)} %bitcast.343), channel_id=1, replica_groups=mesh['cols'=4,'rows'=8] {'rows'}, dimensions={1} | all-to-all | bytes 131072 | tf_op jit(solution)/shard_map/all_to_all | solution.py:52
  135.3 0.6 gather_fusion.3
  136.3 0.6 fusion.4
  136.9 1.4 convolution_bitcast_fusion.4
  138.4 45.0 %all-reduce.14.cloned.1.call-done = f32[128,1024]{1,0:T(8,128)} async-done(((f32[128,1024]{1,0:T(8,128)}), f32[128,1024]{1,0:T(8,128)}) %all-reduce.14.cloned.1.call-update) | async-done | bytes 524304 | tf_op jit(solution)/shard_map/psum | solution.py:60
  183.4 1.5 fusion.46
  184.9 0.8 fusion.21
  185.7 39.6 %all-reduce.3 = (f32[]{:T(128)}, f32[]{:T(128)}, f32[]{:T(128)}) all-reduce(f32[]{:T(128)} %get-tuple-element.21, f32[]{:T(128)} %get-tuple-element.20, f32[]{:T(128)} %get-tuple-element.19), channel_id=1, replica_groups=mesh['cols'=4,'rows'=8] {'cols','rows'}, use_global_device_ids=true, to_apply=%region_10.11 | all-reduce | flops 3 | bytes 24 | tf_op jit(solution)/shard_map/psum | solution.py:70
  227.3 0.6 gather_fusion.4
  227.8 9.3 %all_to_all.43 = bf16[32,8,128]{2,0,1:T(8,128)(2,1)S(1)} all-to-all(bf16[32,8,128]{2,0,1:T(8,128)(2,1)S(1)} %bitcast.344), channel_id=1, replica_groups=mesh['cols'=4,'rows'=8] {'rows'}, dimensions={1} | all-to-all | bytes 131072 | tf_op jit(solution)/shard_map/all_to_all | solution.py:52
  237.1 0.6 gather_fusion.5
  237.8 0.3 fusion.69
  238.1 0.6 fusion.3
  238.6 1.4 convolution_bitcast_fusion.3
  240.2 45.0 %all-reduce.16.cloned.1.call-done = f32[128,1024]{1,0:T(8,128)} async-done(((f32[128,1024]{1,0:T(8,128)}), f32[128,1024]{1,0:T(8,128)}) %all-reduce.16.cloned.1.call-update) | async-done | bytes 524304 | tf_op jit(solution)/shard_map/psum | solution.py:60
  285.2 1.5 fusion.43
  286.6 1.7 multiply_reduce_fusion.5
  288.3 39.6 %all-reduce.2 = (f32[]{:T(128)}, f32[]{:T(128)}, f32[]{:T(128)}) all-reduce(f32[]{:T(128)} %get-tuple-element.13, f32[]{:T(128)} %get-tuple-element.12, f32[]{:T(128)} %get-tuple-element.18), channel_id=1, replica_groups=mesh['cols'=4,'rows'=8] {'cols','rows'}, use_global_device_ids=true, to_apply=%region_17.18 | all-reduce | flops 3 | bytes 24 | tf_op jit(solution)/shard_map/psum | solution.py:70
  329.9 0.6 gather_fusion.6
  330.4 9.3 %all_to_all.44 = bf16[32,8,128]{2,0,1:T(8,128)(2,1)S(1)} all-to-all(bf16[32,8,128]{2,0,1:T(8,128)(2,1)S(1)} %bitcast.345), channel_id=1, replica_groups=mesh['cols'=4,'rows'=8] {'rows'}, dimensions={1} | all-to-all | bytes 131072 | tf_op jit(solution)/shard_map/all_to_all | solution.py:52
  339.7 0.6 gather_fusion.7
  340.7 0.6 fusion.2
  341.3 1.4 convolution_bitcast_fusion.2
  342.8 45.0 %all-reduce.18.cloned.1.call-done = f32[128,1024]{1,0:T(8,128)} async-done(((f32[128,1024]{1,0:T(8,128)}), f32[128,1024]{1,0:T(8,128)}) %all-reduce.18.cloned.1.call-update) | async-done | bytes 524304 | tf_op jit(solution)/shard_map/psum | solution.py:60
  387.8 1.5 fusion.40
  389.2 1.6 fusion.13
  390.8 39.7 %all-reduce.1 = (f32[]{:T(128)}, f32[]{:T(128)}, f32[]{:T(128)}) all-reduce(f32[]{:T(128)} %get-tuple-element.17, f32[]{:T(128)} %get-tuple-element.16, f32[]{:T(128)} %get-tuple-element.15), channel_id=1, replica_groups=mesh['cols'=4,'rows'=8] {'cols','rows'}, use_global_device_ids=true, to_apply=%region_24.25 | all-reduce | flops 3 | bytes 24 | tf_op jit(solution)/shard_map/psum | solution.py:70
  432.7 0.6 gather_fusion.8
  433.2 9.3 %all_to_all.45 = bf16[32,8,128]{2,0,1:T(8,128)(2,1)S(1)} all-to-all(bf16[32,8,128]{2,0,1:T(8,128)(2,1)S(1)} %bitcast.346), channel_id=1, replica_groups=mesh['cols'=4,'rows'=8] {'rows'}, dimensions={1} | all-to-all | bytes 131072 | tf_op jit(solution)/shard_map/all_to_all | solution.py:52
  442.5 0.6 gather_fusion.9
  443.2 0.3 fusion.65
  443.5 0.6 fusion.1
  444.0 1.4 convolution_bitcast_fusion.1
  445.5 45.1 %all-reduce.20.cloned.1.call-done = f32[128,1024]{1,0:T(8,128)} async-done(((f32[128,1024]{1,0:T(8,128)}), f32[128,1024]{1,0:T(8,128)}) %all-reduce.20.cloned.1.call-update) | async-done | bytes 524304 | tf_op jit(solution)/shard_map/psum | solution.py:60
  490.6 1.5 fusion.37
  492.1 1.6 multiply_reduce_fusion.1
  493.6 39.6 %all-reduce = (f32[]{:T(128)}, f32[]{:T(128)}, f32[]{:T(128)}) all-reduce(f32[]{:T(128)} %get-tuple-element.11, f32[]{:T(128)} %get-tuple-element.10, f32[]{:T(128)} %get-tuple-element.14), channel_id=1, replica_groups=mesh['cols'=4,'rows'=8] {'cols','rows'}, use_global_device_ids=true, to_apply=%region_31.32 | all-reduce | flops 3 | bytes 24 | tf_op jit(solution)/shard_map/psum | solution.py:70
  535.2 0.6 gather_fusion.10
  535.8 9.3 %all_to_all.46 = bf16[32,8,128]{2,0,1:T(8,128)(2,1)S(1)} all-to-all(bf16[32,8,128]{2,0,1:T(8,128)(2,1)S(1)} %bitcast.342), channel_id=1, replica_groups=mesh['cols'=4,'rows'=8] {'rows'}, dimensions={1} | all-to-all | bytes 131072 | tf_op jit(solution)/shard_map/all_to_all | solution.py:52
  545.1 0.6 gather_fusion.11
  546.1 0.6 fusion
  546.6 1.4 convolution_bitcast_fusion
  548.1 45.1 %all-reduce.22.cloned.1.call-done = f32[128,1024]{1,0:T(8,128)} async-done(((f32[128,1024]{1,0:T(8,128)}), f32[128,1024]{1,0:T(8,128)}) %all-reduce.22.cloned.1.call-update) | async-done | bytes 524304 | tf_op jit(solution)/shard_map/psum | solution.py:60
  593.2 1.5 multiply_reduce_fusion
  594.7 39.5 %psum.178 = f32[]{:T(128)} all-reduce(f32[]{:T(128)} %multiply_reduce_fusion), channel_id=1, replica_groups=mesh['cols'=4,'rows'=8] {'cols','rows'}, use_global_device_ids=true, to_apply=%region_38.39 | all-reduce | flops 1 | bytes 8 | tf_op jit(solution)/shard_map/psum | solution.py:70
  634.9 0.7 fusion.35
  635.7 1.9 multiply_subtract_fusion
  (49 shorter events, 2.8 us)
Async XLA Ops:
  7.2 8.5 %copy-start = (f32[8,128,128]{2,1,0:T(8,128)S(1)}, f32[8,128,128]{2,1,0:T(8,128)}, u32[]{:S(2)}) copy-start(f32[8,128,128]{2,1,0:T(8,128)} %param.11) | copy-start | bytes 1572868
  7.9 0.7 copy-start.6
  9.3 11.9 %all-to-all-start = ((s32[8,1,1]{2,1,0:T(1,128)}), s32[8,1,1]{2,1,0:T(1,128)S(1)}, u32[]{:S(2)}, u32[]{:S(2)}) async-start(s32[8,1,1]{2,1,0:T(1,128)} %copy.175), calls=%async_computation | async-start | bytes 8192 | tf_op jit(solution)/shard_map/all_to_all | solution.py:35
  15.7 10.4 %copy-start.7 = (s32[4]{0:T(128)S(1)}, s32[4]{0:T(128)}, u32[]{:S(2)}) copy-start(s32[4]{0:T(128)} %param.13) | copy-start | bytes 52
  15.7 16.7 %copy-start.2 = (bf16[4,128,128]{2,1,0:T(8,128)(2,1)S(1)}, bf16[4,128,128]{2,1,0:T(8,128)(2,1)}, u32[]{:S(2)}) copy-start(bf16[4,128,128]{2,1,0:T(8,128)(2,1)} %param.12) | copy-start | bytes 393220
  17.2 15.6 %copy-start.1 = (f32[8,128,128]{2,1,0:T(8,128)S(1)}, f32[8,128,128]{2,1,0:T(8,128)}, u32[]{:S(2)}) copy-start(f32[8,128,128]{2,1,0:T(8,128)} %param.10) | copy-start | bytes 1572868
  22.6 9.2 %all-to-all-start.1 = ((bf16[32,8,128]{2,0,1:T(8,128)(2,1)}), bf16[32,8,128]{2,0,1:T(8,128)(2,1)S(1)}, u32[]{:S(2)}, u32[]{:S(2)}) async-start(bf16[32,8,128]{2,0,1:T(8,128)(2,1)} %bitcast.5), calls=%async_computation.1 | async-start | bytes 131072 | tf_op jit(solution)/shard_map/all_to_all | solution.py:52
  26.0 53.0 %all-reduce.12.cloned.1.call-start = ((), (), s32[]{:S(2)}) async-start(), calls=%async_computation.7 | async-start | bytes 1048576 | tf_op jit(solution)/shard_map/psum | solution.py:60
  32.8 0.7 copy-start.4
  35.0 148.4 %all-reduce.14.cloned.1.call-start = ((), (), s32[]{:S(2)}) async-start(), calls=%async_computation.8 | async-start | bytes 1048576 | tf_op jit(solution)/shard_map/psum | solution.py:60
  35.1 45.4 %copy-start.3 = (f32[32,1024]{1,0:T(8,128)S(1)}, f32[32,1024]{1,0:T(8,128)}, u32[]{:S(2)}) copy-start(f32[32,1024]{1,0:T(8,128)} %param.8) | copy-start | bytes 393220
  138.3 146.9 %all-reduce.16.cloned.1.call-start = ((), (), s32[]{:S(2)}) async-start(), calls=%async_computation.9 | async-start | bytes 1048576 | tf_op jit(solution)/shard_map/psum | solution.py:60
  183.4 1.5 copy-start.5
  240.1 147.7 %all-reduce.18.cloned.1.call-start = ((), (), s32[]{:S(2)}) async-start(), calls=%async_computation.10 | async-start | bytes 1048576 | tf_op jit(solution)/shard_map/psum | solution.py:60
  342.7 147.9 %all-reduce.20.cloned.1.call-start = ((), (), s32[]{:S(2)}) async-start(), calls=%async_computation.11 | async-start | bytes 1048576 | tf_op jit(solution)/shard_map/psum | solution.py:60
  445.5 147.7 %all-reduce.22.cloned.1.call-start = ((), (), s32[]{:S(2)}) async-start(), calls=%async_computation.12 | async-start | bytes 1048576 | tf_op jit(solution)/shard_map/psum | solution.py:60
Sparse Core Ops, SparseCore 0:
  35.1 43.8 all-reduce.11
  138.4 44.9 all-reduce.13
  240.2 44.9 all-reduce.15
  342.8 44.8 all-reduce.17
  445.6 44.9 all-reduce.19
  548.2 44.9 all-reduce.21
where the time goes:
time: 646 us; the launch traced here: 644 us
  blocking collectives  284 us (44%)
  waiting for transfers between devices  279 us (43%)
  between operations  27.4 us (4%)
  matrix products  23.3 us (4%)
  other arithmetic  12 us (2%)
  starting transfers between devices  9.95 us (2%)
  local copies, waits for them, and re-layouts  8.86 us (1%)
    psum x6, waiting for transfers between devices, on_device(): lax.psum(jnp.dot(width_factor, (local_part + coupled).reshape(width_dev,...  269 us
    psum x5, blocking collectives, on_device(): lax.psum((jnp.sum(direction * fisher_dir), jnp.sum(fisher_dir * precond_r...  198 us
    all_to_all x5, blocking collectives, on_device(): lax.all_to_all(rounded[:, granted, :], 'rows', split_axis=1, concat_axis=...  46.4 us
    psum x1, blocking collectives, on_device(): res_norm = lax.psum(jnp.sum(residual * precond_res), ('cols', 'rows'))  39.6 us
  transfers between devices with their start and end apart: 8, of which 8 were waited for; matrix products, arithmetic and copies ran while one was open for 0% of the time, Pallas kernels for 0%

commit v1 on v0

--- a/solution.py
+++ b/solution.py
@@ -57,11 +57,16 @@
             "ekj,kji->eki", sources, coupling_tiles, preferred_element_type=jnp.float32
         )
         coupled = jnp.einsum("eki,kb->ebi", products, placing, precision=highest)
-        summed = lax.psum(
-            jnp.dot(
-                width_factor, (local_part + coupled).reshape(width_dev, rows_dev), precision=highest
+        summed = jnp.sum(
+            lax.all_gather(
+                jnp.dot(
+                    width_factor,
+                    (local_part + coupled).reshape(width_dev, rows_dev),
+                    precision=highest,
+                ),
+                "cols",
             ),
-            "cols",
+            axis=0,
         )
         fisher_dir = lax.dynamic_slice_in_dim(
             summed, lax.axis_index("cols") * width_dev, width_dev, 0

time: 646 us -> 615 us (0.952)
  waiting for transfers between devices: 279 us -> 217 us
  local copies, waits for them, and re-layouts: 8.86 us -> 28.8 us
  other arithmetic: 12 us -> 23.8 us
    psum x6 -> x0, waiting for transfers between devices: 269 us -> none  [on_device(): lax.psum(jnp.dot(width_factor, (local_part + coupled).reshape(width_dev,...]
    all_gather x0 -> x6, waiting for transfers between devices: none -> 207 us  [on_device(): lax.all_gather(jnp.dot(width_factor, (local_part + coupled).reshape(width...]
    reduce_sum x0 -> x6, other arithmetic: none -> 11.9 us  [on_device(): jnp.sum(lax.all_gather(jnp.dot(width_factor, (local_part + coupled).resha...]
    all_gather x0 -> x6, local copies, waits for them, and re-layouts: none -> 11.6 us  [on_device(): lax.all_gather(jnp.dot(width_factor, (local_part + coupled).reshape(width...]
    dynamic_slice x0 -> x6, local copies, waits for them, and re-layouts: none -> 6.7 us  [on_device(): lax.dynamic_slice_in_dim(summed, lax.axis_index('cols') * width_dev, widt...]
where the time goes in v1:
time: 615 us; the launch traced here: 613 us
  blocking collectives  284 us (46%)
  waiting for transfers between devices  217 us (35%)
  local copies, waits for them, and re-layouts  28.8 us (5%)
  between operations  27.7 us (5%)
  other arithmetic  23.8 us (4%)
  matrix products  22.8 us (4%)
  starting transfers between devices  9.95 us (2%)
    all_gather x6, waiting for transfers between devices, on_device(): lax.all_gather(jnp.dot(width_factor, (local_part + coupled).reshape(width...  207 us
    psum x5, blocking collectives, on_device(): lax.psum((jnp.sum(direction * fisher_dir), jnp.sum(fisher_dir * precond_r...  198 us
    all_to_all x5, blocking collectives, on_device(): lax.all_to_all(rounded[:, granted, :], 'rows', split_axis=1, concat_axis=...  46.4 us
    psum x1, blocking collectives, on_device(): res_norm = lax.psum(jnp.sum(residual * precond_res), ('cols', 'rows'))  39.6 us
  transfers between devices with their start and end apart: 8, of which 8 were waited for; matrix products, arithmetic and copies ran while one was open for 0% of the time, Pallas kernels for 0%

profile of v1, /device:TPU:0, one launch (start us, length us, event | category | flops | bytes accessed | tf_op | source)
XLA Modules:
  0.0 613.1 jit_solution(1040607999040789251)
XLA Ops:
  9.3 6.4 %all-to-all-start = ((s32[8,1,1]{2,1,0:T(1,128)}), s32[8,1,1]{2,1,0:T(1,128)S(1)}, u32[]{:S(2)}, u32[]{:S(2)}) async-start(s32[8,1,1]{2,1,0:T(1,128)} %copy.149), calls=%async_computation | async-start | bytes 8192 | tf_op jit(solution)/shard_map/all_to_all | solution.py:35
  15.7 1.5 bitcast_convert_fusion
  17.2 4.0 all-to-all-done
  21.5 1.2 gather_fusion
  22.7 3.4 all-to-all-start.1
  26.1 0.7 fusion.83
  26.8 5.0 all-to-all-done.1
  32.4 1.1 convolution_bitcast_fusion.11
  33.8 1.6 fusion.5
  35.4 1.8 convolution_bitcast_fusion.5
  37.2 33.6 %all-gather.13.cloned.1.call-done = f32[512,1024]{0,1:T(8,128)} async-done(((f32[128,1024]{0,1:T(8,128)}), f32[512,1024]{0,1:T(8,128)}) %all-gather.13.cloned.1.call-update) | async-done | bytes 2097168 | tf_op jit(solution)/shard_map/all_gather | solution.py:61
  70.9 1.9 reshape.220
  72.8 1.2 reduce_sum.213
  75.1 0.7 fusion.25
  75.8 39.6 %all-reduce.4 = (f32[]{:T(128)}, f32[]{:T(128)}, f32[]{:T(128)}) all-reduce(f32[]{:T(128)} %get-tuple-element.20, f32[]{:T(128)} %get-tuple-element.19, f32[]{:T(128)} %get-tuple-element.18), channel_id=1, replica_groups=mesh['cols'=4,'rows'=8] {'cols','rows'}, use_global_device_ids=true, to_apply=%region_1.2 | all-reduce | flops 3 | bytes 24 | tf_op jit(solution)/shard_map/psum | solution.py:47
  119.2 0.7 gather_fusion.2
  119.8 9.3 %all_to_all.42 = bf16[32,8,128]{2,0,1:T(8,128)(2,1)S(1)} all-to-all(bf16[32,8,128]{2,0,1:T(8,128)(2,1)S(1)} %bitcast.355), channel_id=1, replica_groups=mesh['cols'=4,'rows'=8] {'rows'}, dimensions={1} | all-to-all | bytes 131072 | tf_op jit(solution)/shard_map/all_to_all | solution.py:52
  130.8 1.8 convolution_bitcast_fusion.4
  132.7 34.7 %all-gather.15.cloned.1.call-done = f32[512,1024]{0,1:T(8,128)} async-done(((f32[128,1024]{0,1:T(8,128)}), f32[512,1024]{0,1:T(8,128)}) %all-gather.15.cloned.1.call-update) | async-done | bytes 2097168 | tf_op jit(solution)/shard_map/all_gather | solution.py:61
  167.4 1.9 reshape.221
  169.3 2.1 reduce_sum.216
  171.5 1.3 constant_dynamic-slice_fusion.4
  173.5 1.4 fusion.21
  174.8 39.6 %all-reduce.3 = (f32[]{:T(128)}, f32[]{:T(128)}, f32[]{:T(128)}) all-reduce(f32[]{:T(128)} %get-tuple-element.17, f32[]{:T(128)} %get-tuple-element.16, f32[]{:T(128)} %get-tuple-element.15), channel_id=1, replica_groups=mesh['cols'=4,'rows'=8] {'cols','rows'}, use_global_device_ids=true, to_apply=%region_10.11 | all-reduce | flops 3 | bytes 24 | tf_op jit(solution)/shard_map/psum | solution.py:75
  216.3 0.7 fusion.93
  217.0 0.7 gather_fusion.4
  217.7 9.3 %all_to_all.43 = bf16[32,8,128]{2,0,1:T(8,128)(2,1)S(1)} all-to-all(bf16[32,8,128]{2,0,1:T(8,128)(2,1)S(1)} %bitcast.356), channel_id=1, replica_groups=mesh['cols'=4,'rows'=8] {'rows'}, dimensions={1} | all-to-all | bytes 131072 | tf_op jit(solution)/shard_map/all_to_all | solution.py:52
  228.7 1.8 convolution_bitcast_fusion.3
  230.6 34.7 %all-gather.17.cloned.1.call-done = f32[512,1024]{0,1:T(8,128)} async-done(((f32[128,1024]{0,1:T(8,128)}), f32[512,1024]{0,1:T(8,128)}) %all-gather.17.cloned.1.call-update) | async-done | bytes 2097168 | tf_op jit(solution)/shard_map/all_gather | solution.py:61
  265.3 1.9 reshape.222
  267.2 2.1 reduce_sum.220
  269.4 1.3 constant_dynamic-slice_fusion.3
  271.4 1.4 multiply_reduce_fusion.5
  272.8 39.6 %all-reduce.2 = (f32[]{:T(128)}, f32[]{:T(128)}, f32[]{:T(128)}) all-reduce(f32[]{:T(128)} %get-tuple-element.9, f32[]{:T(128)} %get-tuple-element.8, f32[]{:T(128)} %get-tuple-element.14), channel_id=1, replica_groups=mesh['cols'=4,'rows'=8] {'cols','rows'}, use_global_device_ids=true, to_apply=%region_17.18 | all-reduce | flops 3 | bytes 24 | tf_op jit(solution)/shard_map/psum | solution.py:75
  314.4 0.7 gather_fusion.6
  315.1 9.3 %all_to_all.44 = bf16[32,8,128]{2,0,1:T(8,128)(2,1)S(1)} all-to-all(bf16[32,8,128]{2,0,1:T(8,128)(2,1)S(1)} %bitcast.357), channel_id=1, replica_groups=mesh['cols'=4,'rows'=8] {'rows'}, dimensions={1} | all-to-all | bytes 131072 | tf_op jit(solution)/shard_map/all_to_all | solution.py:52
  324.4 0.7 gather_fusion.7
  326.1 1.8 convolution_bitcast_fusion.2
  328.0 34.8 %all-gather.19.cloned.1.call-done = f32[512,1024]{0,1:T(8,128)} async-done(((f32[128,1024]{0,1:T(8,128)}), f32[512,1024]{0,1:T(8,128)}) %all-gather.19.cloned.1.call-update) | async-done | bytes 2097168 | tf_op jit(solution)/shard_map/all_gather | solution.py:61
  362.7 1.9 reshape.223
  364.7 2.1 reduce_sum.224
  366.8 1.3 constant_dynamic-slice_fusion.2
  368.9 1.4 fusion.13
  370.3 39.6 %all-reduce.1 = (f32[]{:T(128)}, f32[]{:T(128)}, f32[]{:T(128)}) all-reduce(f32[]{:T(128)} %get-tuple-element.13, f32[]{:T(128)} %get-tuple-element.12, f32[]{:T(128)} %get-tuple-element.11), channel_id=1, replica_groups=mesh['cols'=4,'rows'=8] {'cols','rows'}, use_global_device_ids=true, to_apply=%region_24.25 | all-reduce | flops 3 | bytes 24 | tf_op jit(solution)/shard_map/psum | solution.py:75
  412.0 0.7 gather_fusion.8
  412.6 9.3 %all_to_all.45 = bf16[32,8,128]{2,0,1:T(8,128)(2,1)S(1)} all-to-all(bf16[32,8,128]{2,0,1:T(8,128)(2,1)S(1)} %bitcast.358), channel_id=1, replica_groups=mesh['cols'=4,'rows'=8] {'rows'}, dimensions={1} | all-to-all | bytes 131072 | tf_op jit(solution)/shard_map/all_to_all | solution.py:52
  423.6 1.8 convolution_bitcast_fusion.1
  425.5 34.8 %all-gather.21.cloned.1.call-done = f32[512,1024]{0,1:T(8,128)} async-done(((f32[128,1024]{0,1:T(8,128)}), f32[512,1024]{0,1:T(8,128)}) %all-gather.21.cloned.1.call-update) | async-done | bytes 2097168 | tf_op jit(solution)/shard_map/all_gather | solution.py:61
  460.2 1.9 reshape.224
  462.2 2.1 reduce_sum.228
  464.3 1.3 constant_dynamic-slice_fusion.1
  466.4 1.3 multiply_reduce_fusion.1
  467.7 39.5 %all-reduce = (f32[]{:T(128)}, f32[]{:T(128)}, f32[]{:T(128)}) all-reduce(f32[]{:T(128)} %get-tuple-element.7, f32[]{:T(128)} %get-tuple-element.6, f32[]{:T(128)} %get-tuple-element.10), channel_id=1, replica_groups=mesh['cols'=4,'rows'=8] {'cols','rows'}, use_global_device_ids=true, to_apply=%region_31.32 | all-reduce | flops 3 | bytes 24 | tf_op jit(solution)/shard_map/psum | solution.py:75
  509.2 0.7 gather_fusion.10
  509.9 9.3 %all_to_all.46 = bf16[32,8,128]{2,0,1:T(8,128)(2,1)S(1)} all-to-all(bf16[32,8,128]{2,0,1:T(8,128)(2,1)S(1)} %bitcast.354), channel_id=1, replica_groups=mesh['cols'=4,'rows'=8] {'rows'}, dimensions={1} | all-to-all | bytes 131072 | tf_op jit(solution)/shard_map/all_to_all | solution.py:52
  520.8 1.8 convolution_bitcast_fusion
  522.7 34.8 %all-gather.23.cloned.1.call-done = f32[512,1024]{0,1:T(8,128)} async-done(((f32[128,1024]{0,1:T(8,128)}), f32[512,1024]{0,1:T(8,128)}) %all-gather.23.cloned.1.call-update) | async-done | bytes 2097168 | tf_op jit(solution)/shard_map/all_gather | solution.py:61
  557.5 1.9 reshape.225
  559.4 2.1 reduce_sum.232
  561.6 1.3 constant_dynamic-slice_fusion
  563.1 1.6 multiply_reduce_fusion
  564.7 39.4 %psum.130 = f32[]{:T(128)} all-reduce(f32[]{:T(128)} %multiply_reduce_fusion), channel_id=1, replica_groups=mesh['cols'=4,'rows'=8] {'cols','rows'}, use_global_device_ids=true, to_apply=%region_38.39 | all-reduce | flops 1 | bytes 8 | tf_op jit(solution)/shard_map/psum | solution.py:75
  604.7 0.7 fusion.35
  605.5 0.7 multiply_subtract_fusion
  (151 shorter events, 14.8 us)
Async XLA Ops:
  7.2 8.5 %copy-start = (f32[8,128,128]{2,1,0:T(8,128)S(1)}, f32[8,128,128]{2,1,0:T(8,128)}, u32[]{:S(2)}) copy-start(f32[8,128,128]{2,1,0:T(8,128)} %param.11) | copy-start | bytes 1572868
  7.2 28.2 %copy-start.37 = (f32[128,32]{0,1:T(8,128)S(1)}, f32[128,32]{0,1:T(8,128)}, u32[]{:S(2)}) copy-start(f32[128,32]{0,1:T(8,128)} %param.9) | copy-start | bytes 49156
  9.3 11.9 %all-to-all-start = ((s32[8,1,1]{2,1,0:T(1,128)}), s32[8,1,1]{2,1,0:T(1,128)S(1)}, u32[]{:S(2)}, u32[]{:S(2)}) async-start(s32[8,1,1]{2,1,0:T(1,128)} %copy.149), calls=%async_computation | async-start | bytes 8192 | tf_op jit(solution)/shard_map/all_to_all | solution.py:35
  21.5 5.3 copy-start.45
  22.7 9.2 %all-to-all-start.1 = ((bf16[32,8,128]{2,0,1:T(8,128)(2,1)}), bf16[32,8,128]{2,0,1:T(8,128)(2,1)S(1)}, u32[]{:S(2)}, u32[]{:S(2)}) async-start(bf16[32,8,128]{2,0,1:T(8,128)(2,1)} %bitcast.5), calls=%async_computation.1 | async-start | bytes 131072 | tf_op jit(solution)/shard_map/all_to_all | solution.py:52
  26.0 44.9 %all-gather.13.cloned.1.call-start = ((), (), s32[]{:S(2)}) async-start(), calls=%async_computation.7 | async-start | bytes 2621440 | tf_op jit(solution)/shard_map/all_gather | solution.py:61
  26.8 6.9 %copy-start.39 = (pred[4,8,1]{1,0,2:T(4,128)(4,1)}, pred[4,8,1]{1,0,2:T(4,128)(4,1)S(1)}, u32[]{:S(2)}) copy-start(pred[4,8,1]{1,0,2:T(4,128)(4,1)S(1)} %fusion.83) | copy-start | bytes 100
  26.8 6.9 %copy-start.46 = (s32[1024]{0:T(1024)}, s32[1024]{0:T(1024)S(1)}, u32[]{:S(2)}) copy-start(s32[1024]{0:T(1024)S(1)} %pad_clamp_fusion) | copy-start | bytes 12292
  37.2 130.2 %all-gather.15.cloned.1.call-start = ((), (), s32[]{:S(2)}) async-start(), calls=%async_computation.8 | async-start | bytes 2621440 | tf_op jit(solution)/shard_map/all_gather | solution.py:61
  74.1 1.0 copy-start.24
  74.1 55.7 %copy-start.2 = (bf16[4,128,128]{2,1,0:T(8,128)(2,1)S(1)}, bf16[4,128,128]{2,1,0:T(8,128)(2,1)}, u32[]{:S(2)}) copy-start(bf16[4,128,128]{2,1,0:T(8,128)(2,1)} %param.12) | copy-start | bytes 393220
  74.1 55.9 %copy-start.40 = (pred[4,8,1]{1,0,2:T(4,128)(4,1)S(1)}, pred[4,8,1]{1,0,2:T(4,128)(4,1)}, u32[]{:S(2)}) copy-start(pred[4,8,1]{1,0,2:T(4,128)(4,1)} %copy-done.39) | copy-start | bytes 100
  74.1 56.1 %copy-start.1 = (f32[8,128,128]{2,1,0:T(8,128)S(1)}, f32[8,128,128]{2,1,0:T(8,128)}, u32[]{:S(2)}) copy-start(f32[8,128,128]{2,1,0:T(8,128)} %param.10) | copy-start | bytes 1572868
  74.5 58.1 %copy-start.5 = (f32[32,1024]{1,0:T(8,128)}, f32[32,1024]{1,0:T(8,128)S(1)}, u32[]{:S(2)}) copy-start(f32[32,1024]{1,0:T(8,128)S(1)} %copy.184) | copy-start | bytes 393220
  119.1 13.5 %copy-start.26 = (f32[32,8,128]{2,0,1:T(8,128)}, f32[32,8,128]{2,0,1:T(8,128)S(1)}, u32[]{:S(2)}) copy-start(f32[32,8,128]{2,0,1:T(8,128)S(1)} %get-tuple-element.51) | copy-start | bytes 393220
  132.6 132.6 %all-gather.17.cloned.1.call-start = ((), (), s32[]{:S(2)}) async-start(), calls=%async_computation.9 | async-start | bytes 2621440 | tf_op jit(solution)/shard_map/all_gather | solution.py:61
  171.4 44.9 %copy-start.27 = (f32[32,8,128]{2,0,1:T(8,128)S(1)}, f32[32,8,128]{2,0,1:T(8,128)}, u32[]{:S(2)}) copy-start(f32[32,8,128]{2,0,1:T(8,128)} %copy-done.26) | copy-start | bytes 393220
  171.4 56.4 %copy-start.41 = (pred[4,8,1]{1,0,2:T(4,128)(4,1)S(1)}, pred[4,8,1]{1,0,2:T(4,128)(4,1)}, u32[]{:S(2)}) copy-start(pred[4,8,1]{1,0,2:T(4,128)(4,1)} %copy-done.39) | copy-start | bytes 100
  172.9 57.6 %copy-start.7 = (f32[32,1024]{1,0:T(8,128)}, f32[32,1024]{1,0:T(8,128)S(1)}, u32[]{:S(2)}) copy-start(f32[32,1024]{1,0:T(8,128)S(1)} %copy.185) | copy-start | bytes 393220
  173.5 57.0 %copy-start.22 = (f32[8,32,128]{2,1,0:T(8,128)}, f32[8,32,128]{2,1,0:T(8,128)S(1)}, u32[]{:S(2)}) copy-start(f32[8,32,128]{2,1,0:T(8,128)S(1)} %fusion.46) | copy-start | bytes 393220
  217.0 13.5 %copy-start.33 = (f32[32,8,128]{2,0,1:T(8,128)}, f32[32,8,128]{2,0,1:T(8,128)S(1)}, u32[]{:S(2)}) copy-start(f32[32,8,128]{2,0,1:T(8,128)S(1)} %get-tuple-element.47) | copy-start | bytes 393220
  230.5 132.2 %all-gather.19.cloned.1.call-start = ((), (), s32[]{:S(2)}) async-start(), calls=%async_computation.10 | async-start | bytes 2621440 | tf_op jit(solution)/shard_map/all_gather | solution.py:61
  269.3 2.1 copy-start.15
  269.4 2.1 copy-start.23
  269.4 45.0 %copy-start.30 = (f32[32,8,128]{2,0,1:T(8,128)S(1)}, f32[32,8,128]{2,0,1:T(8,128)}, u32[]{:S(2)}) copy-start(f32[32,8,128]{2,0,1:T(8,128)} %get-tuple-element.48) | copy-start | bytes 393220
  269.4 45.0 %copy-start.34 = (f32[32,8,128]{2,0,1:T(8,128)S(1)}, f32[32,8,128]{2,0,1:T(8,128)}, u32[]{:S(2)}) copy-start(f32[32,8,128]{2,0,1:T(8,128)} %copy-done.33) | copy-start | bytes 393220
  269.4 55.9 %copy-start.42 = (pred[4,8,1]{1,0,2:T(4,128)(4,1)S(1)}, pred[4,8,1]{1,0,2:T(4,128)(4,1)}, u32[]{:S(2)}) copy-start(pred[4,8,1]{1,0,2:T(4,128)(4,1)} %copy-done.39) | copy-start | bytes 100
  270.8 57.0 %copy-start.9 = (f32[32,1024]{1,0:T(8,128)}, f32[32,1024]{1,0:T(8,128)S(1)}, u32[]{:S(2)}) copy-start(f32[32,1024]{1,0:T(8,128)S(1)} %copy.186) | copy-start | bytes 393220
  271.4 56.5 %copy-start.3 = (f32[8,32,128]{2,1,0:T(8,128)}, f32[8,32,128]{2,1,0:T(8,128)S(1)}, u32[]{:S(2)}) copy-start(f32[8,32,128]{2,1,0:T(8,128)S(1)} %fusion.43) | copy-start | bytes 393220
  327.9 132.3 %all-gather.21.cloned.1.call-start = ((), (), s32[]{:S(2)}) async-start(), calls=%async_computation.11 | async-start | bytes 2621440 | tf_op jit(solution)/shard_map/all_gather | solution.py:61
  366.8 2.1 copy-start.4
  366.8 2.1 copy-start.16
  366.8 2.1 copy-start.28
  366.8 45.1 %copy-start.31 = (f32[32,8,128]{2,0,1:T(8,128)S(1)}, f32[32,8,128]{2,0,1:T(8,128)}, u32[]{:S(2)}) copy-start(f32[32,8,128]{2,0,1:T(8,128)} %get-tuple-element.48) | copy-start | bytes 393220
  368.1 54.6 %copy-start.43 = (pred[4,8,1]{1,0,2:T(4,128)(4,1)S(1)}, pred[4,8,1]{1,0,2:T(4,128)(4,1)}, u32[]{:S(2)}) copy-start(pred[4,8,1]{1,0,2:T(4,128)(4,1)} %copy-done.39) | copy-start | bytes 100
  368.3 55.3 %copy-start.11 = (f32[32,1024]{1,0:T(8,128)}, f32[32,1024]{1,0:T(8,128)S(1)}, u32[]{:S(2)}) copy-start(f32[32,1024]{1,0:T(8,128)S(1)} %copy.187) | copy-start | bytes 393220
  368.9 56.6 %copy-start.20 = (f32[8,32,128]{2,1,0:T(8,128)}, f32[8,32,128]{2,1,0:T(8,128)S(1)}, u32[]{:S(2)}) copy-start(f32[8,32,128]{2,1,0:T(8,128)S(1)} %fusion.40) | copy-start | bytes 393220
  411.9 13.5 %copy-start.35 = (f32[32,8,128]{2,0,1:T(8,128)}, f32[32,8,128]{2,0,1:T(8,128)S(1)}, u32[]{:S(2)}) copy-start(f32[32,8,128]{2,0,1:T(8,128)S(1)} %get-tuple-element.40) | copy-start | bytes 393220
  425.4 132.0 %all-gather.23.cloned.1.call-start = ((), (), s32[]{:S(2)}) async-start(), calls=%async_computation.12 | async-start | bytes 2621440 | tf_op jit(solution)/shard_map/all_gather | solution.py:61
  464.3 2.1 copy-start.18
  464.3 2.1 copy-start.21
  464.3 2.1 copy-start.38
  464.3 44.8 %copy-start.36 = (f32[32,8,128]{2,0,1:T(8,128)S(1)}, f32[32,8,128]{2,0,1:T(8,128)}, u32[]{:S(2)}) copy-start(f32[32,8,128]{2,0,1:T(8,128)} %copy-done.35) | copy-start | bytes 393220
  464.3 55.7 %copy-start.44 = (pred[4,8,1]{1,0,2:T(4,128)(4,1)S(1)}, pred[4,8,1]{1,0,2:T(4,128)(4,1)}, u32[]{:S(2)}) copy-start(pred[4,8,1]{1,0,2:T(4,128)(4,1)} %copy-done.39) | copy-start | bytes 100
  465.8 56.8 %copy-start.13 = (f32[32,1024]{1,0:T(8,128)}, f32[32,1024]{1,0:T(8,128)S(1)}, u32[]{:S(2)}) copy-start(f32[32,1024]{1,0:T(8,128)S(1)} %copy.188) | copy-start | bytes 393220
  559.4 3.7 copy-start.19
  559.4 45.3 %copy-start.17 = (f32[32,1024]{1,0:T(8,128)S(1)}, f32[32,1024]{1,0:T(8,128)}, u32[]{:S(2)}) copy-start(f32[32,1024]{1,0:T(8,128)} %get-tuple-element.49) | copy-start | bytes 393220
  561.6 43.2 %copy-start.29 = (f32[32,1024]{1,0:T(8,128)S(1)}, f32[32,1024]{1,0:T(8,128)}, u32[]{:S(2)}) copy-start(f32[32,1024]{1,0:T(8,128)} %get-tuple-element.45) | copy-start | bytes 393220
  561.6 43.2 %copy-start.32 = (f32[32,1024]{1,0:T(8,128)S(1)}, f32[32,1024]{1,0:T(8,128)}, u32[]{:S(2)}) copy-start(f32[32,1024]{1,0:T(8,128)} %get-tuple-element.38) | copy-start | bytes 393220
  561.6 43.9 %copy-start.6 = (f32[32,1024]{1,0:T(8,128)S(1)}, f32[32,1024]{1,0:T(8,128)}, u32[]{:S(2)}) copy-start(f32[32,1024]{1,0:T(8,128)} %copy-done.5) | copy-start | bytes 393220
  561.6 43.9 %copy-start.8 = (f32[32,1024]{1,0:T(8,128)S(1)}, f32[32,1024]{1,0:T(8,128)}, u32[]{:S(2)}) copy-start(f32[32,1024]{1,0:T(8,128)} %copy-done.7) | copy-start | bytes 393220
  561.6 43.9 %copy-start.10 = (f32[32,1024]{1,0:T(8,128)S(1)}, f32[32,1024]{1,0:T(8,128)}, u32[]{:S(2)}) copy-start(f32[32,1024]{1,0:T(8,128)} %copy-done.9) | copy-start | bytes 393220
  561.6 43.9 %copy-start.12 = (f32[32,1024]{1,0:T(8,128)S(1)}, f32[32,1024]{1,0:T(8,128)}, u32[]{:S(2)}) copy-start(f32[32,1024]{1,0:T(8,128)} %copy-done.11) | copy-start | bytes 393220
  561.6 43.9 %copy-start.14 = (f32[32,1024]{1,0:T(8,128)S(1)}, f32[32,1024]{1,0:T(8,128)}, u32[]{:S(2)}) copy-start(f32[32,1024]{1,0:T(8,128)} %copy-done.13) | copy-start | bytes 393220
  561.6 43.9 %copy-start.25 = (f32[32,1024]{1,0:T(8,128)S(1)}, f32[32,1024]{1,0:T(8,128)}, u32[]{:S(2)}) copy-start(f32[32,1024]{1,0:T(8,128)} %param.8) | copy-start | bytes 393220
Sparse Core Ops, SparseCore 0:
  37.3 33.5 all-gather.12
  132.7 34.5 all-gather.14
  230.6 34.6 all-gather.16
  328.0 34.6 all-gather.18
  425.5 34.6 all-gather.20
  522.8 34.6 all-gather.22
